TPU v7x, 128 devices: a whole 4x4x4 slice. The times are simulated.
128 devices in a mesh: fsdp: 64 (over z, x_hi, y, core), tensor: 2 (over x_lo).
Axes of the slice: x: 4 (x_hi: 2, x_lo: 2; x = x_hi * 2 + x_lo), y: 4, z: 4, core: 2. Of those that a mesh axis runs over, the one named last changes fastest.
Arguments:
- tokens: bfloat16 [8192, 1024], P('fsdp'), may hold values from -6 to 6
- segment: int32 [8192], P('fsdp'), may hold values from 0 to 8191, as said below
- w_query: bfloat16 [1024, 1024], P('fsdp', 'tensor'), may hold values from -0.1875 to 0.1875
- w_key: bfloat16 [1024, 512], P('fsdp', 'tensor'), may hold values from -0.1875 to 0.1875
- w_value: bfloat16 [1024, 512], P('fsdp', 'tensor'), may hold values from -0.1875 to 0.1875
- w_output: bfloat16 [1024, 1024], P('tensor', 'fsdp'), may hold values from -0.5 to 0.5
- w_gate: bfloat16 [1024, 4608], P('fsdp', 'tensor'), may hold values from -0.1875 to 0.1875
- w_up: bfloat16 [1024, 4608], P('fsdp', 'tensor'), may hold values from -0.1875 to 0.1875
- w_down: bfloat16 [4608, 1024], P('tensor', 'fsdp'), may hold values from -0.09375 to 0.09375
- norm_attn: bfloat16 [1024], P('fsdp'), may hold values from 0.25 to 1.75
- norm_ffn: bfloat16 [1024], P('fsdp'), may hold values from 0.25 to 1.75
- norm_query: bfloat16 [64], P('fsdp'), may hold values from 0.25 to 1.75
- norm_key: bfloat16 [64], P('fsdp'), may hold values from 0.25 to 1.75
- cotangent: bfloat16 [8192, 1024], P('fsdp'), may hold values from -16 to 16
Outputs:
- block_out: bfloat16 [8192, 1024], P('fsdp')
- grad_tokens: bfloat16 [8192, 1024], P('fsdp')
- grad_query: float32 [1024, 1024], P('fsdp', 'tensor')
- grad_key: float32 [1024, 512], P('fsdp', 'tensor')
- grad_value: float32 [1024, 512], P('fsdp', 'tensor')
- grad_output: float32 [1024, 1024], P('tensor', 'fsdp')
- grad_gate: float32 [1024, 4608], P('fsdp', 'tensor')
- grad_up: float32 [1024, 4608], P('fsdp', 'tensor')
- grad_down: float32 [4608, 1024], P('tensor', 'fsdp')
- grad_norm_attn: float32 [1024], P('fsdp')
- grad_norm_ffn: float32 [1024], P('fsdp')
- grad_norm_query: float32 [64], P('fsdp')
- grad_norm_key: float32 [64], P('fsdp')
Inputs may be any that keep to these rules, and one draw needn't show every extreme that they name: `segment`: ids never fall; all tokens of an id lie in one aligned block of 128 tokens; the first and the last token of every such block start a new id.
All inputs are finite; a program needn't handle non-finite values.
Results may differ from a plain program's by a relative error of at most 0.019.
Values may be sent and summed in bfloat16 or wider, within the bound.
No kernel may reach another device: no remote copies, remote signals or barrier semaphores. Data moves between devices by JAX's collectives and lax.ppermute only.
A program may use at most 128 MiB of HBM per device.

v0:
```python
import jax
import jax.numpy as jnp
from jax import lax
from jax.sharding import PartitionSpec as P

epsilon = 1e-05
rope_base = 1000000.0


def matmul(matrix, second):
    return jnp.dot(matrix, second, preferred_element_type=jnp.float32)


def matmul_tr(matrix, second):
    return lax.dot_general(
        matrix, second, (((1,), (1,)), ((), ())), preferred_element_type=jnp.float32
    )


def tr_matmul(matrix, second):
    return lax.dot_general(
        matrix, second, (((0,), (0,)), ((), ())), preferred_element_type=jnp.float32
    )


def contract(pattern, matrix, second):
    return jnp.einsum(pattern, matrix, second, preferred_element_type=jnp.float32)


def normalize(vector):
    inverse = lax.rsqrt(jnp.mean(vector * vector, axis=-1, keepdims=True) + epsilon)
    return (vector * inverse, inverse)


def norm_back(grad_in, normed, inverse):
    return inverse * (grad_in - normed * jnp.mean(grad_in * normed, axis=-1, keepdims=True))


def rotate(vector):
    half_size = vector.shape[-1] // 2
    return jnp.concatenate([-vector[..., half_size:], vector[..., :half_size]], axis=-1)


def rotate_back(vector):
    half_size = vector.shape[-1] // 2
    return jnp.concatenate([vector[..., half_size:], -vector[..., :half_size]], axis=-1)


def tables(segment, head_size):
    row_count = segment.shape[0]
    row_index = jnp.arange(row_count, dtype=jnp.int32)
    same_segment = segment[:, None] == segment[None, :]
    first_row = jnp.min(jnp.where(same_segment, row_index[None, :], row_count), axis=1)
    position = (row_index - first_row).astype(jnp.float32)
    allowed = same_segment & (row_index[None, :] <= row_index[:, None])
    half_size = head_size // 2
    frequency = jnp.power(rope_base, -2.0 * jnp.arange(half_size, dtype=jnp.float32) / head_size)
    phase_angle = position[:, None] * frequency[None, :]
    phase_angle = jnp.concatenate([phase_angle, phase_angle], axis=1)
    return (allowed, jnp.cos(phase_angle)[:, None, :], jnp.sin(phase_angle)[:, None, :])


def head_prep(raw_heads, head_gain, cos_table, sin_table):
    unit_heads, inverse = normalize(raw_heads)
    scaled = unit_heads * head_gain
    return (scaled * cos_table + rotate(scaled) * sin_table, unit_heads, inverse)


def head_back(grad_in, unit_heads, inverse, head_gain, cos_table, sin_table):
    grad_scaled = grad_in * cos_table + rotate_back(grad_in * sin_table)
    gain_grad = jnp.sum(grad_scaled * unit_heads, axis=(0, 1))
    return (norm_back(grad_scaled * head_gain, unit_heads, inverse), gain_grad)


def score_block(query_heads, key_heads, allowed):
    row_count, head_count, head_size = query_heads.shape
    kv_count = key_heads.shape[1]
    query_groups = query_heads.reshape(row_count, kv_count, head_count // kv_count, head_size)
    scores = contract("ikgd,jkd->kgij", query_groups, key_heads) * head_size ** (-0.5)
    return (query_groups, jnp.where(allowed, scores, -1e30))


def attend(query_heads, key_heads, value_heads, allowed):
    row_count, head_count, head_size = query_heads.shape
    query_groups, masked = score_block(query_heads, key_heads, allowed)
    row_max = jnp.max(masked, axis=-1, keepdims=True)
    exp_scores = jnp.exp(masked - row_max)
    denominator = jnp.sum(exp_scores, axis=-1, keepdims=True)
    log_total = row_max + jnp.log(denominator)
    attn_weights = (exp_scores / denominator).astype(jnp.bfloat16)
    mixed = contract("kgij,jkd->ikgd", attn_weights, value_heads).astype(jnp.bfloat16)
    return (mixed.reshape(row_count, head_count * head_size), log_total)


def attend_back(query_heads, key_heads, value_heads, attended, grad_attended, log_total, allowed):
    row_count, head_count, head_size = query_heads.shape
    kv_count = key_heads.shape[1]
    group_size = head_count // kv_count
    query_groups, masked = score_block(query_heads, key_heads, allowed)
    prob = jnp.exp(masked - log_total)
    prob_low = prob.astype(jnp.bfloat16)
    grad_groups = grad_attended.reshape(row_count, kv_count, group_size, head_size)
    out_groups = attended.reshape(row_count, kv_count, group_size, head_size)
    row_delta = jnp.sum(grad_groups.astype(jnp.float32) * out_groups.astype(jnp.float32), axis=-1)
    row_delta = jnp.transpose(row_delta, (1, 2, 0))[..., None]
    grad_kv_value = contract("kgij,ikgd->jkd", prob_low, grad_groups)
    grad_prob = contract("ikgd,jkd->kgij", grad_groups, value_heads)
    grad_scores = (prob * (grad_prob - row_delta) * head_size ** (-0.5)).astype(jnp.bfloat16)
    grad_query = contract("kgij,jkd->ikgd", grad_scores, key_heads).reshape(
        row_count, head_count, head_size
    )
    grad_key = contract("kgij,ikgd->jkd", grad_scores, query_groups)
    return (grad_query, grad_key, grad_kv_value)


def on_device(
    tokens,
    segment,
    w_query,
    w_key,
    w_value,
    w_output,
    w_gate,
    w_up,
    w_down,
    norm_attn,
    norm_ffn,
    norm_query,
    norm_key,
    cotangent,
):
    shards = (
        w_query,
        w_key,
        w_value,
        w_gate,
        w_up,
        w_output,
        w_down,
        norm_attn,
        norm_ffn,
        norm_query,
        norm_key,
    )
    gathered = (
        lax.all_gather(shards[0], "fsdp", axis=0, tiled=True),
        lax.all_gather(shards[1], "fsdp", axis=0, tiled=True),
        lax.all_gather(shards[2], "fsdp", axis=0, tiled=True),
        lax.all_gather(shards[3], "fsdp", axis=0, tiled=True),
        lax.all_gather(shards[4], "fsdp", axis=0, tiled=True),
        lax.all_gather(shards[5], "fsdp", axis=1, tiled=True),
        lax.all_gather(shards[6], "fsdp", axis=1, tiled=True),
        lax.all_gather(shards[7], "fsdp", axis=0, tiled=True),
        lax.all_gather(shards[8], "fsdp", axis=0, tiled=True),
        lax.all_gather(shards[9], "fsdp", axis=0, tiled=True),
        lax.all_gather(shards[10], "fsdp", axis=0, tiled=True),
    )
    (
        full_query,
        full_key,
        full_value,
        full_gate,
        full_up,
        full_output,
        full_down,
        gain_attn,
        gain_ffn,
        gain_query,
        gain_key,
    ) = gathered
    row_count = tokens.shape[0]
    head_size = gain_query.shape[0]
    head_count = full_query.shape[1] // head_size
    kv_count = full_key.shape[1] // head_size
    allowed, cos_table, sin_table = tables(segment, head_size)
    inputs = tokens.astype(jnp.float32)
    normed_one, inv_one = normalize(inputs)
    hidden_one = (normed_one * gain_attn).astype(jnp.bfloat16)
    query_raw = matmul(hidden_one, full_query).reshape(row_count, head_count, head_size)
    key_raw = matmul(hidden_one, full_key).reshape(row_count, kv_count, head_size)
    value_heads = (
        matmul(hidden_one, full_value).astype(jnp.bfloat16).reshape(row_count, kv_count, head_size)
    )
    query_rot, query_unit, query_inv = head_prep(query_raw, gain_query, cos_table, sin_table)
    key_rot, key_unit, key_inv = head_prep(key_raw, gain_key, cos_table, sin_table)
    query_heads = query_rot.astype(jnp.bfloat16)
    key_heads = key_rot.astype(jnp.bfloat16)
    attended, log_total = attend(query_heads, key_heads, value_heads, allowed)
    residual = inputs + lax.psum(matmul(attended, full_output), "tensor")
    normed_two, inv_two = normalize(residual)
    hidden_two = (normed_two * gain_ffn).astype(jnp.bfloat16)
    gate_pre = matmul(hidden_two, full_gate)
    up_pre = matmul(hidden_two, full_up)
    sigmoid_gate = jax.nn.sigmoid(gate_pre)
    activation = (gate_pre * sigmoid_gate * up_pre).astype(jnp.bfloat16)
    ffn_result = lax.psum(matmul(activation, full_down).astype(jnp.bfloat16), "tensor").astype(
        jnp.float32
    )
    block_out = (residual + ffn_result).astype(jnp.bfloat16)
    (
        back_query,
        back_key,
        back_value,
        back_gate,
        back_up,
        back_output,
        back_down,
        back_attn,
        back_ffn,
        back_qgain,
        back_kgain,
    ) = gathered
    grad_act = matmul_tr(cotangent, back_down)
    grad_gate_pre = (
        grad_act * up_pre * sigmoid_gate * (1.0 + gate_pre * (1.0 - sigmoid_gate))
    ).astype(jnp.bfloat16)
    grad_up_pre = (grad_act * gate_pre * sigmoid_gate).astype(jnp.bfloat16)
    partial_two = matmul_tr(grad_gate_pre, back_gate) + matmul_tr(grad_up_pre, back_up)
    grad_hidden_two = lax.psum(partial_two, "tensor")
    grad_norm_ffn = jnp.sum(grad_hidden_two * normed_two, axis=0)
    ffn_width = grad_gate_pre.shape[1]
    grad_residual = cotangent.astype(jnp.float32) + norm_back(
        grad_hidden_two * back_ffn, normed_two, inv_two
    )
    grad_res_low = grad_residual.astype(jnp.bfloat16)
    grad_attended = matmul_tr(grad_res_low, back_output).astype(jnp.bfloat16)
    grad_q_rot, grad_k_rot, grad_kv_value = attend_back(
        query_heads, key_heads, value_heads, attended, grad_attended, log_total, allowed
    )
    grad_q_raw, part_norm_query = head_back(
        grad_q_rot, query_unit, query_inv, back_qgain, cos_table, sin_table
    )
    grad_k_raw, part_norm_key = head_back(
        grad_k_rot, key_unit, key_inv, back_kgain, cos_table, sin_table
    )
    query_low = grad_q_raw.reshape(row_count, head_count * head_size).astype(jnp.bfloat16)
    key_low = grad_k_raw.reshape(row_count, kv_count * head_size).astype(jnp.bfloat16)
    value_low = grad_kv_value.reshape(row_count, kv_count * head_size).astype(jnp.bfloat16)
    partial_one = (
        matmul_tr(query_low, back_query)
        + matmul_tr(key_low, back_key)
        + matmul_tr(value_low, back_value)
    )
    grad_hidden_one, grad_norm_query, grad_norm_key = lax.psum(
        (partial_one, part_norm_query, part_norm_key), "tensor"
    )
    grad_norm_attn = jnp.sum(grad_hidden_one * normed_one, axis=0)
    grad_tokens = (
        grad_residual + norm_back(grad_hidden_one * back_attn, normed_one, inv_one)
    ).astype(jnp.bfloat16)
    query_width = query_low.shape[1]
    key_width = key_low.shape[1]
    whole_owned = lax.psum_scatter(
        jnp.concatenate(
            [
                jnp.concatenate(
                    [
                        tr_matmul(hidden_one, query_low),
                        tr_matmul(hidden_one, key_low),
                        tr_matmul(hidden_one, value_low),
                        tr_matmul(grad_res_low, attended),
                    ],
                    axis=1,
                ),
                jnp.concatenate(
                    [
                        tr_matmul(hidden_two, grad_gate_pre),
                        tr_matmul(hidden_two, grad_up_pre),
                        tr_matmul(cotangent, activation),
                    ],
                    axis=1,
                ),
            ],
            axis=1,
        ),
        "fsdp",
        scatter_dimension=0,
        tiled=True,
    )
    attn_width = 2 * query_width + 2 * key_width
    attn_owned = whole_owned[:, :attn_width]
    ffn_owned = whole_owned[:, attn_width:]
    gain_owned = (
        lax.psum_scatter(grad_norm_attn, "fsdp", scatter_dimension=0, tiled=True),
        lax.psum_scatter(grad_norm_ffn, "fsdp", scatter_dimension=0, tiled=True),
        lax.psum_scatter(grad_norm_query, "fsdp", scatter_dimension=0, tiled=True),
        lax.psum_scatter(grad_norm_key, "fsdp", scatter_dimension=0, tiled=True),
    )
    grad_query = attn_owned[:, :query_width]
    grad_key = attn_owned[:, query_width : query_width + key_width]
    grad_value = attn_owned[:, query_width + key_width : query_width + 2 * key_width]
    grad_output = attn_owned[:, query_width + 2 * key_width :].T
    grad_gate = ffn_owned[:, :ffn_width]
    grad_up = ffn_owned[:, ffn_width : 2 * ffn_width]
    grad_down = ffn_owned[:, 2 * ffn_width :].T
    return (
        block_out,
        grad_tokens,
        grad_query,
        grad_key,
        grad_value,
        grad_output,
        grad_gate,
        grad_up,
        grad_down,
        gain_owned[0],
        gain_owned[1],
        gain_owned[2],
        gain_owned[3],
    )


def solution(mesh):
    return jax.shard_map(
        on_device,
        mesh=mesh,
        in_specs=(
            P("fsdp", None),
            P("fsdp"),
            P("fsdp", "tensor"),
            P("fsdp", "tensor"),
            P("fsdp", "tensor"),
            P("tensor", "fsdp"),
            P("fsdp", "tensor"),
            P("fsdp", "tensor"),
            P("tensor", "fsdp"),
            P("fsdp"),
            P("fsdp"),
            P("fsdp"),
            P("fsdp"),
            P("fsdp", None),
        ),
        out_specs=(
            P("fsdp", None),
            P("fsdp", None),
            P("fsdp", "tensor"),
            P("fsdp", "tensor"),
            P("fsdp", "tensor"),
            P("tensor", "fsdp"),
            P("fsdp", "tensor"),
            P("fsdp", "tensor"),
            P("tensor", "fsdp"),
            P("fsdp"),
            P("fsdp"),
            P("fsdp"),
            P("fsdp"),
        ),
        check_vma=False,
    )
```

profile of v0, /device:TPU:0, one launch (start us, length us, event | category | flops | bytes accessed | tf_op | source)
XLA Modules:
  0.0 1088.6 jit_solution(5932731994119234216)
XLA Ops:
  17.2 173.2 %all-reduce.10 = (bf16[1024]{0:T(1024)(128)(2,1)S(1)}, bf16[64]{0:T(256)(128)(2,1)S(1)}, bf16[64]{0:T(256)(128)(2,1)S(1)}, bf16[1024]{0:T(1024)(128)(2,1)S(1)}) all-reduce(bf16[1024]{0:T(1024)(128)(2,1)S(1)} %dynamic-update-slice, bf16[64]{0:T(256)(128)(2,1)S(1)} %dynamic-update-slice.1, ...), channel_id=1, replica_groups=mesh['fsdp'=64,'tensor'=2] {'fsdp'}, use_global_device_ids=true, to_apply=%add | all-reduce | flops 2176 | bytes 8704
  190.6 89.9 %all_gather.35 = bf16[1024,256]{1,0:T(8,128)(2,1)S(1)} all-gather(bf16[16,256]{1,0:T(8,128)(2,1)} %param.17), channel_id=1, replica_groups=mesh['fsdp'=64,'tensor'=2] {'fsdp'}, dimensions={0}, use_global_device_ids=true | all-gather | bytes 532480 | tf_op jit(solution)/shard_map/all_gather | solution.py:147
  282.0 91.7 %all_gather.34 = bf16[1024,256]{1,0:T(8,128)(2,1)S(1)} all-gather(bf16[16,256]{1,0:T(8,128)(2,1)} %param.18), channel_id=1, replica_groups=mesh['fsdp'=64,'tensor'=2] {'fsdp'}, dimensions={0}, use_global_device_ids=true | all-gather | bytes 532480 | tf_op jit(solution)/shard_map/all_gather | solution.py:148
  376.8 1.7 fusion.37
  379.6 2.5 fusion.47
  386.3 25.0 %all-reduce.16.cloned.1.call-done = f32[128,1024]{1,0:T(8,128)} async-done(((f32[128,1024]{1,0:T(8,128)}), f32[128,1024]{1,0:T(8,128)}) %all-reduce.16.cloned.1.call-update) | async-done | bytes 524304 | tf_op jit(solution)/shard_map/psum | solution.py:189
  413.2 75.6 %all-gather.12.cloned.1.call-done = bf16[1024,2304]{1,0:T(8,128)(2,1)} async-done(((bf16[16,2304]{1,0:T(8,128)(2,1)}), bf16[1024,2304]{1,0:T(8,128)(2,1)}) %all-gather.12.cloned.1.call-update) | async-done | bytes 4718608 | tf_op jit(solution)/shard_map/all_gather | solution.py:150
  488.8 4.2 fusion.49
  492.9 70.8 %all-gather.10.cloned.1.call-done = bf16[1024,2304]{1,0:T(8,128)(2,1)} async-done(((bf16[16,2304]{1,0:T(8,128)(2,1)}), bf16[1024,2304]{1,0:T(8,128)(2,1)}) %all-gather.10.cloned.1.call-update) | async-done | bytes 4718608 | tf_op jit(solution)/shard_map/all_gather | solution.py:149
  563.7 4.1 fusion.48
  567.9 70.8 %all-gather.14.cloned.1.call-done = bf16[2304,1024]{0,1:T(8,128)(2,1)} async-done(((bf16[2304,16]{0,1:T(8,128)(2,1)}), bf16[2304,1024]{0,1:T(8,128)(2,1)}) %all-gather.14.cloned.1.call-update) | async-done | bytes 4718608 | tf_op jit(solution)/shard_map/all_gather | solution.py:152
  638.7 5.1 multiply_convert_fusion
  645.5 4.8 convolution_add_fusion.1
  651.6 4.9 convolution_convert_fusion
  656.8 27.3 %all-reduce.20.cloned.1.call-done = f32[128,1024]{1,0:T(8,128)} async-done(((f32[128,1024]{1,0:T(8,128)}), f32[128,1024]{1,0:T(8,128)}) %all-reduce.20.cloned.1.call-update) | async-done | bytes 524304 | tf_op jit(solution)/shard_map/psum | solution.py:219
  684.1 1.9 multiply_reduce_fusion
  686.5 31.4 %all-reduce.18.cloned.1.call-done = bf16[128,1024]{1,0:T(8,128)(2,1)} async-done(((bf16[128,1024]{1,0:T(8,128)(2,1)}), bf16[128,1024]{1,0:T(8,128)(2,1)}) %all-reduce.18.cloned.1.call-update) | async-done | bytes 262160 | tf_op jit(solution)/shard_map/psum | solution.py:196
  717.9 2.2 multiply_add_fusion
  725.1 2.1 fusion.53
  734.9 1.9 convolution_dynamic-update-slice_fusion.3
  736.8 2.5 fusion
  740.8 2.3 convolution_dynamic-update-slice_fusion.4
  743.1 1.9 convolution_dynamic-update-slice_fusion.2
  745.0 5.1 convolution_dynamic-update-slice_fusion.1
  750.1 5.0 convolution_dynamic-update-slice_fusion
  755.2 5.1 bitcast_dynamic-update-slice_fusion
  760.3 15.3 %all-reduce.22.cloned.1.call-done = f32[128,1024]{1,0:T(8,128)} async-done(((f32[128,1024]{1,0:T(8,128)}), f32[128,1024]{1,0:T(8,128)}) %all-reduce.22.cloned.1.call-update) | async-done | bytes 524304 | tf_op jit(solution)/shard_map/psum | solution.py:244
  777.0 174.7 %all-reduce.8 = (f32[1024]{0:T(1024)S(1)}, f32[1024]{0:T(1024)S(1)}, f32[64]{0:T(128)S(1)}, f32[64]{0:T(128)S(1)}) all-reduce(f32[1024]{0:T(1024)S(1)} %get-tuple-element.15, f32[1024]{0:T(1024)S(1)} %copy-done.19, f32[64]{0:T(128)S(1)} %get-tuple-element.17, f32[64]{0:T(128)S(1)} %copy-done.25), channel_id=3, replica_groups=mesh['fsdp'=64,'tensor'=2] {'fsdp'}, use_global_device_ids=true, to_apply=%region_18.19.clone | all-reduce | flops 2176 | bytes 17408
  954.8 5.6 all-reduce.9
  961.6 2.0 fusion.17
  963.6 113.6 %reduce-scatter.2.cloned.1.call-done = f32[16,8448]{1,0:T(8,128)} async-done(((f32[1024,8448]{1,0:T(8,128)}), f32[16,8448]{1,0:T(8,128)}) %reduce-scatter.2.cloned.1.call-update) | async-done | bytes 540688 | tf_op jit(solution)/shard_map/reduce_scatter | solution.py:253
  1079.9 1.8 slice_bitcast_fusion
  (154 shorter events, 45.2 us)
Async XLA Ops:
  7.2 369.6 %all-gather.6.cloned.1.call-start = ((), (), s32[]{:S(2)}) async-start(), calls=%async_computation.1 | async-start | bytes 1064960 | tf_op jit(solution)/shard_map/all_gather | solution.py:146
  7.9 371.7 %all-gather.8.cloned.1.call-start = ((), (), s32[]{:S(2)}) async-start(), calls=%async_computation.2 | async-start | bytes 1064960 | tf_op jit(solution)/shard_map/all_gather | solution.py:151
  8.7 402.7 %all-reduce.16.cloned.1.call-start = ((), (), s32[]{:S(2)}) async-start(), calls=%async_computation.3 | async-start | bytes 1048576 | tf_op jit(solution)/shard_map/psum | solution.py:189
  12.0 366.6 %copy-start.16 = (f32[128]{0:T(128)}, f32[128]{0:T(128)S(1)}, u32[]{:S(2)}) copy-start(f32[128]{0:T(128)S(1)} %add_rsqrt_fusion.3) | copy-start | bytes 1540
  190.4 188.4 %copy-start.20 = (f32[64]{0:T(128)}, f32[64]{0:T(128)S(1)}, u32[]{:S(2)}) copy-start(f32[64]{0:T(128)S(1)} %convert_element_type.115) | copy-start | bytes 772
  190.4 188.9 %copy-start.21 = (f32[64]{0:T(128)}, f32[64]{0:T(128)S(1)}, u32[]{:S(2)}) copy-start(f32[64]{0:T(128)S(1)} %convert_element_type.118) | copy-start | bytes 772
  375.8 6.3 copy-start.14
  378.6 32.7 %copy-start = (bf16[128,1024]{1,0:T(8,128)(2,1)S(1)}, bf16[128,1024]{1,0:T(8,128)(2,1)}, u32[]{:S(2)}) copy-start(bf16[128,1024]{1,0:T(8,128)(2,1)} %param.14) | copy-start | bytes 786436
  379.2 5.4 copy-start.15
  379.3 5.3 copy-start.18
  379.6 33.0 %copy-start.9 = (bf16[4,64,2,128]{3,1,2,0:T(8,128)(2,1)}, bf16[4,64,2,128]{3,1,2,0:T(8,128)(2,1)S(1)}, u32[]{:S(2)}) copy-start(bf16[4,64,2,128]{3,1,2,0:T(8,128)(2,1)S(1)} %convolution_convert_fusion.2) | copy-start | bytes 393220
  382.2 106.6 %all-gather.12.cloned.1.call-start = ((), (), s32[]{:S(2)}) async-start(), calls=%async_computation.5 | async-start | bytes 4792320 | tf_op jit(solution)/shard_map/all_gather | solution.py:150
  382.8 181.0 %all-gather.10.cloned.1.call-start = ((), (), s32[]{:S(2)}) async-start(), calls=%async_computation.4 | async-start | bytes 4792320 | tf_op jit(solution)/shard_map/all_gather | solution.py:149
  383.3 255.3 %all-gather.14.cloned.1.call-start = ((), (), s32[]{:S(2)}) async-start(), calls=%async_computation.6 | async-start | bytes 4792320 | tf_op jit(solution)/shard_map/all_gather | solution.py:152
  383.9 300.2 %all-reduce.20.cloned.1.call-start = ((), (), s32[]{:S(2)}) async-start(), calls=%async_computation.8 | async-start | bytes 1048576 | tf_op jit(solution)/shard_map/psum | solution.py:219
  413.2 225.5 %copy-start.11 = (bf16[128,1024]{1,0:T(8,128)(2,1)S(1)}, bf16[128,1024]{1,0:T(8,128)(2,1)}, u32[]{:S(2)}) copy-start(bf16[128,1024]{1,0:T(8,128)(2,1)} %param.27) | copy-start | bytes 786436
  638.7 5.1 copy-start.1
  650.3 33.8 %copy-start.24 = (f32[128]{0:T(128)S(1)}, f32[128]{0:T(128)}, u32[]{:S(2)}) copy-start(f32[128]{0:T(128)} %copy-done.23) | copy-start | bytes 1540
  650.3 67.6 %all-reduce.18.cloned.1.call-start = ((), (), s32[]{:S(2)}) async-start(), calls=%async_computation.7 | async-start | bytes 524288 | tf_op jit(solution)/shard_map/psum | solution.py:196
  656.5 119.1 %all-reduce.22.cloned.1.call-start = ((), (), s32[]{:S(2)}) async-start(), calls=%async_computation.9 | async-start | bytes 1048576 | tf_op jit(solution)/shard_map/psum | solution.py:244
  721.7 9.7 copy-start.22
  723.6 5.8 copy-start.13
  725.1 9.8 copy-start.17
  730.6 6.3 copy-start.2
  733.6 9.6 copy-start.10
  736.8 8.2 copy-start.7
  739.4 337.8 %reduce-scatter.2.cloned.1.call-start = ((), (), s32[]{:S(2)}) async-start(), calls=%async_computation.10 | async-start | bytes 35143680 | tf_op jit(solution)/shard_map/reduce_scatter | solution.py:253
  745.0 5.1 copy-start.5
  750.1 5.1 copy-start.3
  750.1 5.1 copy-start.12
  760.3 16.6 %copy-start.19 = (f32[1024]{0:T(1024)S(1)}, f32[1024]{0:T(1024)}, u32[]{:S(2)}) copy-start(f32[1024]{0:T(1024)} %get-tuple-element.13) | copy-start | bytes 12292
  760.3 16.6 %copy-start.25 = (f32[64]{0:T(128)S(1)}, f32[64]{0:T(128)}, u32[]{:S(2)}) copy-start(f32[64]{0:T(128)} %get-tuple-element.19) | copy-start | bytes 772
  (4 other events, 4.6 us)
Sparse Core Ops, SparseCore 0:
  11.3 68.3 all-gather.5
  83.1 62.7 all-gather.7
  382.3 28.9 all-reduce.15
  414.9 73.8 all-gather.11
  492.3 71.3 all-gather.9
  567.3 71.3 all-gather.13
  650.4 33.6 all-reduce.19
  687.1 30.7 all-reduce.17
  739.5 36.1 all-reduce.21
  781.9 295.2 reduce-scatter.1
where the time goes:
time: 1090 us
  blocking collectives  535 us (49%)
  waiting for transfers between devices  433 us (40%)
  matrix products  64.5 us (6%)
  other arithmetic  19.2 us (2%)
  local copies, waits for them, and re-layouts  18.9 us (2%)
  between operations  17.3 us (2%)
    unnamed x2, blocking collectives  348 us
    reduce_scatter x1, waiting for transfers between devices, on_device(): lax.psum_scatter(jnp.concatenate([jnp.concatenate([tr_matmul(hidden_one,...  114 us
    all_gather x1, blocking collectives, on_device(): lax.all_gather(shards[2], 'fsdp', axis=0, tiled=True)  91.7 us
    all_gather x1, blocking collectives, on_device(): lax.all_gather(shards[1], 'fsdp', axis=0, tiled=True)  89.9 us
    all_gather x1, waiting for transfers between devices, on_device(): lax.all_gather(shards[4], 'fsdp', axis=0, tiled=True)  75.6 us
    all_gather x1, waiting for transfers between devices, on_device(): lax.all_gather(shards[6], 'fsdp', axis=1, tiled=True)  70.8 us
    all_gather x1, waiting for transfers between devices, on_device(): lax.all_gather(shards[3], 'fsdp', axis=0, tiled=True)  70.8 us
    psum x1, waiting for transfers between devices, on_device(): lax.psum(matmul(activation, full_down).astype(jnp.bfloat16), 'tensor')  31.4 us
  transfers between devices with their start and end apart: 10, of which 8 were waited for; matrix products, arithmetic and copies ran while one was open for 6% of the time, Pallas kernels for 0%

commit v1 on v0

--- a/solution.py
+++ b/solution.py
@@ -145,7 +145,9 @@
     gathered = (
         lax.all_gather(shards[0], "fsdp", axis=0, tiled=True),
         lax.all_gather(shards[1], "fsdp", axis=0, tiled=True),
-        lax.all_gather(shards[2], "fsdp", axis=0, tiled=True),
+        jnp.concatenate(
+            lax.all_to_all(jnp.stack([shards[2]] * lax.axis_size("fsdp")), "fsdp", 0, 0), axis=0
+        ),
         lax.all_gather(shards[3], "fsdp", axis=0, tiled=True),
         lax.all_gather(shards[4], "fsdp", axis=0, tiled=True),
         lax.all_gather(shards[5], "fsdp", axis=1, tiled=True),

time: 1090 us -> 1010 us (0.927)
  blocking collectives: 535 us -> 442 us
  starting transfers between devices: 0.57 us -> 12.1 us
    all_gather x1 -> x0, blocking collectives: 91.7 us -> none  [on_device(): lax.all_gather(shards[2], 'fsdp', axis=0, tiled=True)]
    all_to_all x0 -> x1, starting transfers between devices: none -> 11.5 us  [on_device(): lax.all_to_all(jnp.stack([shards[2]] * lax.axis_size('fsdp')), 'fsdp', 0, 0)]
  transfers between devices with their start and end apart: 10 -> 11, of which waited for: 8 -> 8; matrix products, arithmetic and copies ran while one was open for 6% -> 6% of each run, Pallas kernels for 0% -> 0%
where the time goes in v1:
time: 1010 us
  blocking collectives  442 us (44%)
  waiting for transfers between devices  434 us (43%)
  matrix products  64.6 us (6%)
  local copies, waits for them, and re-layouts  19.6 us (2%)
  other arithmetic  19.2 us (2%)
  between operations  17.4 us (2%)
  starting transfers between devices  12.1 us (1%)
    unnamed x2, blocking collectives  347 us
    reduce_scatter x1, waiting for transfers between devices, on_device(): lax.psum_scatter(jnp.concatenate([jnp.concatenate([tr_matmul(hidden_one,...  114 us
    all_gather x1, blocking collectives, on_device(): lax.all_gather(shards[1], 'fsdp', axis=0, tiled=True)  89.9 us
    all_gather x1, waiting for transfers between devices, on_device(): lax.all_gather(shards[4], 'fsdp', axis=0, tiled=True)  75.6 us
    all_gather x1, waiting for transfers between devices, on_device(): lax.all_gather(shards[6], 'fsdp', axis=1, tiled=True)  70.8 us
    all_gather x1, waiting for transfers between devices, on_device(): lax.all_gather(shards[3], 'fsdp', axis=0, tiled=True)  70.8 us
    psum x1, waiting for transfers between devices, on_device(): lax.psum(matmul(activation, full_down).astype(jnp.bfloat16), 'tensor')  31.4 us
    psum x1, waiting for transfers between devices, on_device(): grad_hidden_two = lax.psum(partial_two, 'tensor')  27.3 us
  transfers between devices with their start and end apart: 11, of which 8 were waited for; matrix products, arithmetic and copies ran while one was open for 6% of the time, Pallas kernels for 0%

profile of v1, /device:TPU:0, one launch (start us, length us, event | category | flops | bytes accessed | tf_op | source)
XLA Modules:
  0.0 1009.4 jit_solution(2245898893422974511)
XLA Ops:
  9.5 11.5 %all-to-all-start = ((bf16[64,16,256]{2,1,0:T(8,128)(2,1)}), bf16[64,16,256]{2,1,0:T(8,128)(2,1)S(1)}, u32[]{:S(2)}, u32[]{:S(2)}) async-start(bf16[64,16,256]{2,1,0:T(8,128)(2,1)} %stack.2), calls=%async_computation | async-start | bytes 1048576 | tf_op jit(solution)/shard_map/all_to_all | solution.py:149
  31.1 172.0 %all-reduce.10 = (bf16[1024]{0:T(1024)(128)(2,1)S(1)}, bf16[64]{0:T(256)(128)(2,1)S(1)}, bf16[64]{0:T(256)(128)(2,1)S(1)}, bf16[1024]{0:T(1024)(128)(2,1)S(1)}) all-reduce(bf16[1024]{0:T(1024)(128)(2,1)S(1)} %dynamic-update-slice, bf16[64]{0:T(256)(128)(2,1)S(1)} %dynamic-update-slice.1, ...), channel_id=1, replica_groups=mesh['fsdp'=64,'tensor'=2] {'fsdp'}, use_global_device_ids=true, to_apply=%add | all-reduce | flops 2176 | bytes 8704
  203.1 89.9 %all_gather.31 = bf16[1024,256]{1,0:T(8,128)(2,1)S(1)} all-gather(bf16[16,256]{1,0:T(8,128)(2,1)} %param.17), channel_id=1, replica_groups=mesh['fsdp'=64,'tensor'=2] {'fsdp'}, dimensions={0}, use_global_device_ids=true | all-gather | bytes 532480 | tf_op jit(solution)/shard_map/all_gather | solution.py:147
  299.1 2.5 fusion.47
  305.8 26.3 %all-reduce.16.cloned.1.call-done = f32[128,1024]{1,0:T(8,128)} async-done(((f32[128,1024]{1,0:T(8,128)}), f32[128,1024]{1,0:T(8,128)}) %all-reduce.16.cloned.1.call-update) | async-done | bytes 524304 | tf_op jit(solution)/shard_map/psum | solution.py:191
  334.0 75.6 %all-gather.12.cloned.1.call-done = bf16[1024,2304]{1,0:T(8,128)(2,1)} async-done(((bf16[16,2304]{1,0:T(8,128)(2,1)}), bf16[1024,2304]{1,0:T(8,128)(2,1)}) %all-gather.12.cloned.1.call-update) | async-done | bytes 4718608 | tf_op jit(solution)/shard_map/all_gather | solution.py:152
  409.6 4.2 fusion.49
  413.7 70.8 %all-gather.10.cloned.1.call-done = bf16[1024,2304]{1,0:T(8,128)(2,1)} async-done(((bf16[16,2304]{1,0:T(8,128)(2,1)}), bf16[1024,2304]{1,0:T(8,128)(2,1)}) %all-gather.10.cloned.1.call-update) | async-done | bytes 4718608 | tf_op jit(solution)/shard_map/all_gather | solution.py:151
  484.5 4.2 fusion.48
  488.7 70.8 %all-gather.14.cloned.1.call-done = bf16[2304,1024]{0,1:T(8,128)(2,1)} async-done(((bf16[2304,16]{0,1:T(8,128)(2,1)}), bf16[2304,1024]{0,1:T(8,128)(2,1)}) %all-gather.14.cloned.1.call-update) | async-done | bytes 4718608 | tf_op jit(solution)/shard_map/all_gather | solution.py:154
  559.5 5.1 multiply_convert_fusion
  564.6 1.6 fusion.50
  566.3 4.8 convolution_add_fusion.1
  572.4 4.9 convolution_convert_fusion
  577.6 27.3 %all-reduce.20.cloned.1.call-done = f32[128,1024]{1,0:T(8,128)} async-done(((f32[128,1024]{1,0:T(8,128)}), f32[128,1024]{1,0:T(8,128)}) %all-reduce.20.cloned.1.call-update) | async-done | bytes 524304 | tf_op jit(solution)/shard_map/psum | solution.py:221
  604.9 1.9 multiply_reduce_fusion
  607.3 31.4 %all-reduce.18.cloned.1.call-done = bf16[128,1024]{1,0:T(8,128)(2,1)} async-done(((bf16[128,1024]{1,0:T(8,128)(2,1)}), bf16[128,1024]{1,0:T(8,128)(2,1)}) %all-reduce.18.cloned.1.call-update) | async-done | bytes 262160 | tf_op jit(solution)/shard_map/psum | solution.py:198
  638.7 2.2 multiply_add_fusion
  645.9 2.1 fusion.53
  655.7 1.9 convolution_dynamic-update-slice_fusion.3
  657.7 2.5 fusion
  661.7 2.3 convolution_dynamic-update-slice_fusion.4
  664.0 1.8 convolution_dynamic-update-slice_fusion.2
  665.8 5.0 convolution_dynamic-update-slice_fusion.1
  670.8 5.0 convolution_dynamic-update-slice_fusion
  675.8 5.2 bitcast_dynamic-update-slice_fusion
  681.1 15.4 %all-reduce.22.cloned.1.call-done = f32[128,1024]{1,0:T(8,128)} async-done(((f32[128,1024]{1,0:T(8,128)}), f32[128,1024]{1,0:T(8,128)}) %all-reduce.22.cloned.1.call-update) | async-done | bytes 524304 | tf_op jit(solution)/shard_map/psum | solution.py:246
  697.8 174.7 %all-reduce.8 = (f32[1024]{0:T(1024)S(1)}, f32[1024]{0:T(1024)S(1)}, f32[64]{0:T(128)S(1)}, f32[64]{0:T(128)S(1)}) all-reduce(f32[1024]{0:T(1024)S(1)} %get-tuple-element.15, f32[1024]{0:T(1024)S(1)} %copy-done.19, f32[64]{0:T(128)S(1)} %get-tuple-element.17, f32[64]{0:T(128)S(1)} %copy-done.25), channel_id=3, replica_groups=mesh['fsdp'=64,'tensor'=2] {'fsdp'}, use_global_device_ids=true, to_apply=%region_18.19.clone | all-reduce | flops 2176 | bytes 17408
  875.7 5.6 all-reduce.9
  882.4 2.0 fusion.17
  884.4 113.6 %reduce-scatter.2.cloned.1.call-done = f32[16,8448]{1,0:T(8,128)} async-done(((f32[1024,8448]{1,0:T(8,128)}), f32[16,8448]{1,0:T(8,128)}) %reduce-scatter.2.cloned.1.call-update) | async-done | bytes 540688 | tf_op jit(solution)/shard_map/reduce_scatter | solution.py:255
  1000.8 1.8 slice_bitcast_fusion
  (156 shorter events, 46.1 us)
Async XLA Ops:
  7.2 289.2 %copy-start = (bf16[128,1024]{1,0:T(8,128)(2,1)S(1)}, bf16[128,1024]{1,0:T(8,128)(2,1)}, u32[]{:S(2)}) copy-start(bf16[128,1024]{1,0:T(8,128)(2,1)} %param.14) | copy-start | bytes 786436
  7.2 289.1 %all-gather.6.cloned.1.call-start = ((), (), s32[]{:S(2)}) async-start(), calls=%async_computation.2 | async-start | bytes 1064960 | tf_op jit(solution)/shard_map/all_gather | solution.py:146
  9.5 285.3 %all-to-all-start = ((bf16[64,16,256]{2,1,0:T(8,128)(2,1)}), bf16[64,16,256]{2,1,0:T(8,128)(2,1)S(1)}, u32[]{:S(2)}, u32[]{:S(2)}) async-start(bf16[64,16,256]{2,1,0:T(8,128)(2,1)} %stack.2), calls=%async_computation | async-start | bytes 1048576 | tf_op jit(solution)/shard_map/all_to_all | solution.py:149
  21.0 278.1 %all-gather.8.cloned.1.call-start = ((), (), s32[]{:S(2)}) async-start(), calls=%async_computation.3 | async-start | bytes 1064960 | tf_op jit(solution)/shard_map/all_gather | solution.py:153
  21.7 310.4 %all-reduce.16.cloned.1.call-start = ((), (), s32[]{:S(2)}) async-start(), calls=%async_computation.4 | async-start | bytes 1048576 | tf_op jit(solution)/shard_map/psum | solution.py:191
  25.9 272.2 %copy-start.16 = (f32[128]{0:T(128)}, f32[128]{0:T(128)S(1)}, u32[]{:S(2)}) copy-start(f32[128]{0:T(128)S(1)} %add_rsqrt_fusion.3) | copy-start | bytes 1540
  203.1 95.2 %copy-start.20 = (f32[64]{0:T(128)}, f32[64]{0:T(128)S(1)}, u32[]{:S(2)}) copy-start(f32[64]{0:T(128)S(1)} %convert_element_type.117) | copy-start | bytes 772
  296.3 5.3 copy-start.14
  298.6 5.4 copy-start.15
  298.8 5.3 copy-start.18
  299.0 34.3 %copy-start.9 = (bf16[4,64,2,128]{3,1,2,0:T(8,128)(2,1)}, bf16[4,64,2,128]{3,1,2,0:T(8,128)(2,1)S(1)}, u32[]{:S(2)}) copy-start(bf16[4,64,2,128]{3,1,2,0:T(8,128)(2,1)S(1)} %convolution_convert_fusion.2) | copy-start | bytes 393220
  301.6 107.9 %all-gather.12.cloned.1.call-start = ((), (), s32[]{:S(2)}) async-start(), calls=%async_computation.6 | async-start | bytes 4792320 | tf_op jit(solution)/shard_map/all_gather | solution.py:152
  302.2 182.3 %all-gather.10.cloned.1.call-start = ((), (), s32[]{:S(2)}) async-start(), calls=%async_computation.5 | async-start | bytes 4792320 | tf_op jit(solution)/shard_map/all_gather | solution.py:151
  302.8 256.7 %all-gather.14.cloned.1.call-start = ((), (), s32[]{:S(2)}) async-start(), calls=%async_computation.7 | async-start | bytes 4792320 | tf_op jit(solution)/shard_map/all_gather | solution.py:154
  303.4 301.5 %all-reduce.20.cloned.1.call-start = ((), (), s32[]{:S(2)}) async-start(), calls=%async_computation.9 | async-start | bytes 1048576 | tf_op jit(solution)/shard_map/psum | solution.py:221
  334.0 225.5 %copy-start.11 = (bf16[128,1024]{1,0:T(8,128)(2,1)S(1)}, bf16[128,1024]{1,0:T(8,128)(2,1)}, u32[]{:S(2)}) copy-start(bf16[128,1024]{1,0:T(8,128)(2,1)} %param.27) | copy-start | bytes 786436
  559.5 5.2 copy-start.1
  571.1 33.8 %copy-start.24 = (f32[128]{0:T(128)S(1)}, f32[128]{0:T(128)}, u32[]{:S(2)}) copy-start(f32[128]{0:T(128)} %copy-done.23) | copy-start | bytes 1540
  571.1 67.6 %all-reduce.18.cloned.1.call-start = ((), (), s32[]{:S(2)}) async-start(), calls=%async_computation.8 | async-start | bytes 524288 | tf_op jit(solution)/shard_map/psum | solution.py:198
  577.3 119.2 %all-reduce.22.cloned.1.call-start = ((), (), s32[]{:S(2)}) async-start(), calls=%async_computation.10 | async-start | bytes 1048576 | tf_op jit(solution)/shard_map/psum | solution.py:246
  642.5 9.7 copy-start.22
  644.4 5.8 copy-start.13
  645.9 9.8 copy-start.17
  651.3 6.3 copy-start.2
  654.4 9.6 copy-start.10
  657.7 8.1 copy-start.7
  660.2 337.8 %reduce-scatter.2.cloned.1.call-start = ((), (), s32[]{:S(2)}) async-start(), calls=%async_computation.11 | async-start | bytes 35143680 | tf_op jit(solution)/shard_map/reduce_scatter | solution.py:255
  665.8 5.0 copy-start.5
  670.8 5.0 copy-start.3
  670.8 5.0 copy-start.12
  681.0 16.8 %copy-start.19 = (f32[1024]{0:T(1024)S(1)}, f32[1024]{0:T(1024)}, u32[]{:S(2)}) copy-start(f32[1024]{0:T(1024)} %get-tuple-element.13) | copy-start | bytes 12292
  681.0 16.8 %copy-start.25 = (f32[64]{0:T(128)S(1)}, f32[64]{0:T(128)}, u32[]{:S(2)}) copy-start(f32[64]{0:T(128)} %get-tuple-element.19) | copy-start | bytes 772
  (5 other events, 9.5 us)
Sparse Core Ops, SparseCore 0:
  11.4 68.9 all-gather.5
  83.6 62.6 all-gather.7
  301.7 30.3 all-reduce.15
  335.6 73.8 all-gather.11
  413.1 71.3 all-gather.9
  488.0 71.3 all-gather.13
  571.2 33.6 all-reduce.19
  607.9 30.7 all-reduce.17
  660.3 36.1 all-reduce.21
  702.8 295.2 reduce-scatter.1
